TPU v7x, 32 devices: a whole 2x2x4 slice. The times are simulated.
32 devices in a mesh: group: 2 (over x), shard: 16 (over z, y, core).
Axes of the slice: x: 2, y: 2, z: 4, core: 2. Of those that a mesh axis runs over, the one named last changes fastest.
Arguments:
- offer_attribute_matrix: bfloat16 [128, 128, 1024], P(('group', 'shard')), may hold values from -6 to 6
- kept_offers: int32 [128, 32], P(('group', 'shard')), may hold values from 0 to 127, as said below
- expert_target: int32 [128, 6], P(('group', 'shard')), may hold values from 0 to 15, all different within a row; in each aligned block of 4 rows (0 to 3, 4 to 7, ...) at most 3 rows name the same one
- sequence_extent: int32 [128], P(('group', 'shard')), may hold values from 1 to 128
- behaviour_sequence: bfloat16 [128, 128, 512], P(('group', 'shard')), may hold values from -6 to 6
- inner_projection_matrix: bfloat16 [1024, 1024], replicated, may hold values from -0.1875 to 0.1875
- student_rating_vector: bfloat16 [1024], replicated, may hold values from -0.1875 to 0.1875
- asking_matrix: bfloat16 [16, 1024, 512], P('shard'), may hold values from -0.1875 to 0.1875
- lookup_matrix: bfloat16 [16, 512, 512], P('shard'), may hold values from -0.25 to 0.25
- content_matrix: bfloat16 [16, 512, 512], P('shard'), may hold values from -0.25 to 0.25
- expert_rating_vector: bfloat16 [16, 512], P('shard'), may hold values from -1.1953125 to 1.1953125
Outputs:
- grad_hidden: float32 [1024, 1024], P('shard')
- grad_score: float32 [1024], replicated
Inputs may be any that keep to these rules, and one draw needn't show every extreme that they name: `kept_offers`: the 32 survivors of a request are distinct candidates. `expert_target`: each request names 6 distinct experts; the requests of one device name any expert at most 3 times, a bound that some block reaches.
All inputs are finite; a program needn't handle non-finite values.
Results may differ from a plain program's by a relative error of at most 0.005.
Values may be sent and summed in bfloat16 or wider, within the bound.
No kernel may reach another device: no remote copies, remote signals or barrier semaphores. Data moves between devices by JAX's collectives and lax.ppermute only.
A program may use at most 128 MiB of HBM per device.

v0:
```python
import jax
import jax.numpy as jnp
from jax import lax
from jax.sharding import PartitionSpec as P

ATTENDER_GANGS = 8


def body(
    offer_attribute_matrix,
    kept_offers,
    expert_target,
    sequence_extent,
    behaviour_sequence,
    inner_projection_matrix,
    student_rating_vector,
    asking_matrix,
    lookup_matrix,
    content_matrix,
    expert_rating_vector,
):
    requests_here, offer_number, attribute_span = offer_attribute_matrix.shape
    kept_number = kept_offers.shape[1]
    hist_slots, focus_span = (behaviour_sequence.shape[1], behaviour_sequence.shape[2])
    rankers_each = expert_target.shape[1]
    ranker_count = lax.axis_size("shard")
    routed_rows = requests_here * rankers_each
    capacity = max(2, (routed_rows + ranker_count - 1) // ranker_count + 1)
    place_number = ranker_count * capacity
    row_dest = expert_target.reshape(routed_rows)
    by_expert = (row_dest[:, None] == jnp.arange(ranker_count, dtype=jnp.int32)[None, :]).astype(
        jnp.int32
    )
    earlier = jnp.cumsum(by_expert, axis=0) - by_expert
    rank_in = jnp.sum(earlier * by_expert, axis=1)
    slot_of = row_dest * capacity + rank_in
    placing = slot_of[:, None] == jnp.arange(place_number, dtype=jnp.int32)[None, :]
    placing = placing.reshape(requests_here, rankers_each, place_number)
    placing_b = placing.astype(jnp.bfloat16)
    placing_f = placing.astype(jnp.float32)
    chosen_lines = (
        kept_offers[:, :, None] == jnp.arange(offer_number, dtype=jnp.int32)[None, None, :]
    ).astype(jnp.bfloat16)
    chosen = jnp.einsum(
        "rkc,rcf->rkf", chosen_lines, offer_attribute_matrix, preferred_element_type=jnp.float32
    ).astype(jnp.bfloat16)
    send_rows = jnp.einsum(
        "rts,rkf->skf", placing_b, chosen, preferred_element_type=jnp.float32
    ).astype(jnp.bfloat16)
    send_hist = jnp.einsum(
        "rts,rjf->sjf", placing_b, behaviour_sequence, preferred_element_type=jnp.float32
    ).astype(jnp.bfloat16)
    send_len = jnp.einsum("rts,r->s", placing_f, sequence_extent.astype(jnp.float32)).astype(
        jnp.bfloat16
    )
    arriving_lines, recv_hist, recv_len = (
        lax.all_to_all(send_rows, "shard", split_axis=0, concat_axis=0, tiled=True),
        lax.all_to_all(send_hist, "shard", split_axis=0, concat_axis=0, tiled=True),
        lax.all_to_all(send_len, "shard", split_axis=0, concat_axis=0, tiled=True),
    )
    single_attender_span = focus_span // ATTENDER_GANGS
    segment_places = 16
    segment_number = place_number // segment_places

    def ranker_block(block):
        rows, hist_rows, lens = block
        queries = jnp.dot(
            rows.reshape(-1, attribute_span), asking_matrix[0], preferred_element_type=jnp.float32
        )
        queries = queries.astype(jnp.bfloat16).reshape(
            segment_places, kept_number, ATTENDER_GANGS, single_attender_span
        )
        flat_hist = hist_rows.reshape(-1, focus_span)
        key_rows = jnp.dot(flat_hist, lookup_matrix[0], preferred_element_type=jnp.float32)
        key_rows = key_rows.astype(jnp.bfloat16).reshape(
            segment_places, hist_slots, ATTENDER_GANGS, single_attender_span
        )
        value_rows = jnp.dot(flat_hist, content_matrix[0], preferred_element_type=jnp.float32)
        value_rows = value_rows.astype(jnp.bfloat16).reshape(
            segment_places, hist_slots, ATTENDER_GANGS, single_attender_span
        )
        logits = jnp.einsum(
            "skhd,sjhd->shkj", queries, key_rows, preferred_element_type=jnp.float32
        ) * single_attender_span ** (-0.5)
        lengths = jnp.maximum(lens.astype(jnp.float32), jnp.float32(1.0))
        visible = (
            jnp.arange(hist_slots, dtype=jnp.float32)[None, None, None, :]
            < lengths[:, None, None, None]
        )
        weights = jnp.where(visible, jnp.exp(logits), jnp.float32(0.0))
        attn_probs = (weights / jnp.sum(weights, axis=-1, keepdims=True)).astype(jnp.bfloat16)
        mixed_context = jnp.einsum(
            "shkj,sjhd->skhd", attn_probs, value_rows, preferred_element_type=jnp.float32
        )
        mixed_context = mixed_context.reshape(segment_places, kept_number, focus_span)
        return jnp.sum(mixed_context * expert_rating_vector[0].astype(jnp.float32), axis=-1)

    mentor_output = lax.map(
        ranker_block,
        (
            arriving_lines.reshape(segment_number, segment_places, kept_number, attribute_span),
            recv_hist.reshape(segment_number, segment_places, hist_slots, focus_span),
            recv_len.reshape(segment_number, segment_places),
        ),
    )
    mentor_output = mentor_output.reshape(place_number, kept_number)
    returned = lax.all_to_all(mentor_output, "shard", split_axis=0, concat_axis=0, tiled=True)
    own_teacher = (
        jnp.einsum("rts,sk->rk", placing_f, returned, precision=lax.Precision.HIGHEST)
        / rankers_each
    )
    score_vec = student_rating_vector.astype(jnp.float32)
    flat_feats = offer_attribute_matrix.reshape(requests_here * offer_number, attribute_span)
    preact = jnp.dot(flat_feats, inner_projection_matrix, preferred_element_type=jnp.float32)
    hidden = jnp.maximum(preact, jnp.float32(0.0))
    scores = jnp.sum(hidden * score_vec, axis=-1).reshape(requests_here, offer_number)
    exp_scores = jnp.exp(scores)
    student = exp_scores / jnp.sum(exp_scores, axis=-1, keepdims=True)
    exp_teacher = jnp.exp(own_teacher)
    target = exp_teacher / jnp.sum(exp_teacher, axis=-1, keepdims=True)
    target_cand = jnp.sum(target[:, :, None] * chosen_lines.astype(jnp.float32), axis=1)
    score_grad = (student - target_cand).reshape(requests_here * offer_number, 1)
    hidden_grad = (score_grad * score_vec * (preact > 0).astype(jnp.float32)).astype(jnp.bfloat16)
    local_score = jnp.sum(score_grad * hidden, axis=0)
    grad_rows = lax.psum_scatter(
        lax.dot_general(
            flat_feats, hidden_grad, (((0,), (0,)), ((), ())), preferred_element_type=jnp.float32
        ),
        "shard",
        scatter_dimension=0,
        tiled=True,
    )
    grad_hidden = lax.psum(grad_rows, "group")
    grad_score = lax.psum(local_score, ("group", "shard"))
    return (grad_hidden, grad_score)


def solution(mesh):
    placed = (
        P(("group", "shard"), None, None),
        P(("group", "shard"), None),
        P(("group", "shard"), None),
        P(("group", "shard")),
        P(("group", "shard"), None, None),
        P(),
        P(),
        P("shard", None, None),
        P("shard", None, None),
        P("shard", None, None),
        P("shard", None),
    )
    return jax.shard_map(
        body, mesh=mesh, in_specs=placed, out_specs=(P("shard", None), P()), check_vma=False
    )
```

profile of v0, /device:TPU:0, one launch (start us, length us, event | category | flops | bytes accessed | tf_op | source)
XLA Modules:
  0.0 495.7 jit_solution(17073846660387039856)
XLA Ops:
  10.8 7.4 %all-to-all-start.1 = ((bf16[16,3,1]{1,2,0:T(2,128)(2,1)}), bf16[16,3,1]{1,2,0:T(2,128)(2,1)S(1)}, u32[]{:S(2)}, u32[]{:S(2)}) async-start(bf16[16,3,1]{1,2,0:T(2,128)(2,1)} %all_to_all.27), calls=%async_computation.1 | async-start | bytes 16384 | tf_op jit(solution)/shard_map/all_to_all | solution.py:59
  24.6 5.8 %all-to-all-start.2 = ((bf16[48,32,1024]{2,1,0:T(8,128)(2,1)}), bf16[48,32,1024]{2,1,0:T(8,128)(2,1)}, u32[]{:S(2)}, u32[]{:S(2)}) async-start(bf16[48,32,1024]{2,1,0:T(8,128)(2,1)} %copy.50), calls=%async_computation.2 | async-start | bytes 6291456 | tf_op jit(solution)/shard_map/all_to_all | solution.py:57
  32.3 6.3 %copy.47 = bf16[48,128,512]{2,1,0:T(8,128)(2,1)} copy(bf16[48,128,512]{2,0,1:T(8,128)(2,1)S(1)} %convolution_convert_fusion.3) | data formatting | bytes 12582912 | tf_op jit(solution)/shard_map/convert_element_type | solution.py:52
  38.6 51.1 %all-to-all-done.2 = bf16[48,32,1024]{2,1,0:T(8,128)(2,1)} async-done(((bf16[48,32,1024]{2,1,0:T(8,128)(2,1)}), bf16[48,32,1024]{2,1,0:T(8,128)(2,1)}, u32[]{:S(2)}, u32[]{:S(2)}) %all-to-all-start.2) | async-done | bytes 3145760 | tf_op jit(solution)/shard_map/all_to_all | solution.py:57
  89.7 15.5 %all-to-all-start = ((bf16[48,128,512]{2,1,0:T(8,128)(2,1)}), bf16[48,128,512]{2,1,0:T(8,128)(2,1)}, u32[]{:S(2)}, u32[]{:S(2)}) async-start(bf16[48,128,512]{2,1,0:T(8,128)(2,1)} %copy.47), calls=%async_computation | async-start | bytes 12582912 | tf_op jit(solution)/shard_map/all_to_all | solution.py:58
  108.0 111.3 %all-to-all-done = bf16[48,128,512]{2,1,0:T(8,128)(2,1)} async-done(((bf16[48,128,512]{2,1,0:T(8,128)(2,1)}), bf16[48,128,512]{2,1,0:T(8,128)(2,1)}, u32[]{:S(2)}, u32[]{:S(2)}) %all-to-all-start) | async-done | bytes 6291488 | tf_op jit(solution)/shard_map/all_to_all | solution.py:58
  219.3 107.4 %while.10 = (s32[]{:T(128)}, f32[3,16,32]{2,1,0:T(8,128)S(1)}, bf16[3,16,128,512]{3,2,1,0:T(8,128)(2,1)}, bf16[1,512,512]{2,1,0:T(8,128)(2,1)}, bf16[3,16]{1,0:T...) while((s32[]{:T(128)}, f32[3,16,32]{2,1,0:T(8,128)S(1)}, ...), condition=%wide.region_9.10_spmd, body=%wide.region_6.9_spmd.sunk | while | flops 2825123840 | bytes 61932960 | solution.py:98
  225.1 6.2 %reshape.149 = bf16[16,128,8,64]{3,2,1,0:T(8,128)(2,1)} reshape(bf16[2048,512]{1,0:T(8,128)(2,1)} %convolution_convert_fusion.10) | data formatting | bytes 4194304 | tf_op jit(solution)/shard_map/while/body/eval_jaxpr/reshape | solution.py:75
  236.0 6.0 %fusion.64 = (f32[16,8,32]{2,1,0:T(8,128)S(1)}, f32[16,8,32,128]{3,2,1,0:T(8,128)}) fusion(pred[16,128]{1,0:T(8,128)(4,1)S(1)} %iota_compare_fusion.6, bf16[16,128,8,64]{3,2,1,0:T(8,128)(2,1)} %reshape.149, bf16[16,32,8,64]{3,2,1,0:T(8,128)(2,1)S(1)} %reshape.150), kind=kOutput, calls=%fused_computation.9.clone.1 | convolution fusion | flops 68677632 | bytes 4737024 | tf_op jit(solution)/shard_map/while/body/eval_jaxpr/skhd,sjhd->shkj/dot_general | solution.py:82
  244.6 6.2 %reshape.148 = bf16[16,128,8,64]{3,2,1,0:T(8,128)(2,1)} reshape(bf16[2048,512]{1,0:T(8,128)(2,1)} %convolution_convert_fusion.9) | data formatting | bytes 4194304 | tf_op jit(solution)/shard_map/while/body/eval_jaxpr/reshape | solution.py:79
  250.8 4.2 multiply_reduce_fusion.5
  260.8 6.2 %reshape.149 = bf16[16,128,8,64]{3,2,1,0:T(8,128)(2,1)} reshape(bf16[2048,512]{1,0:T(8,128)(2,1)} %convolution_convert_fusion.10) | data formatting | bytes 4194304 | tf_op jit(solution)/shard_map/while/body/eval_jaxpr/reshape | solution.py:75
  271.8 6.0 %fusion.64 = (f32[16,8,32]{2,1,0:T(8,128)S(1)}, f32[16,8,32,128]{3,2,1,0:T(8,128)}) fusion(pred[16,128]{1,0:T(8,128)(4,1)S(1)} %iota_compare_fusion.6, bf16[16,128,8,64]{3,2,1,0:T(8,128)(2,1)} %reshape.149, bf16[16,32,8,64]{3,2,1,0:T(8,128)(2,1)S(1)} %reshape.150), kind=kOutput, calls=%fused_computation.9.clone.1 | convolution fusion | flops 68677632 | bytes 4737024 | tf_op jit(solution)/shard_map/while/body/eval_jaxpr/skhd,sjhd->shkj/dot_general | solution.py:82
  280.4 6.2 %reshape.148 = bf16[16,128,8,64]{3,2,1,0:T(8,128)(2,1)} reshape(bf16[2048,512]{1,0:T(8,128)(2,1)} %convolution_convert_fusion.9) | data formatting | bytes 4194304 | tf_op jit(solution)/shard_map/while/body/eval_jaxpr/reshape | solution.py:79
  296.6 6.2 %reshape.149 = bf16[16,128,8,64]{3,2,1,0:T(8,128)(2,1)} reshape(bf16[2048,512]{1,0:T(8,128)(2,1)} %convolution_convert_fusion.10) | data formatting | bytes 4194304 | tf_op jit(solution)/shard_map/while/body/eval_jaxpr/reshape | solution.py:75
  307.6 6.0 %fusion.64 = (f32[16,8,32]{2,1,0:T(8,128)S(1)}, f32[16,8,32,128]{3,2,1,0:T(8,128)}) fusion(pred[16,128]{1,0:T(8,128)(4,1)S(1)} %iota_compare_fusion.6, bf16[16,128,8,64]{3,2,1,0:T(8,128)(2,1)} %reshape.149, bf16[16,32,8,64]{3,2,1,0:T(8,128)(2,1)S(1)} %reshape.150), kind=kOutput, calls=%fused_computation.9.clone.1 | convolution fusion | flops 68677632 | bytes 4737024 | tf_op jit(solution)/shard_map/while/body/eval_jaxpr/skhd,sjhd->shkj/dot_general | solution.py:82
  316.2 6.2 %reshape.148 = bf16[16,128,8,64]{3,2,1,0:T(8,128)(2,1)} reshape(bf16[2048,512]{1,0:T(8,128)(2,1)} %convolution_convert_fusion.9) | data formatting | bytes 4194304 | tf_op jit(solution)/shard_map/while/body/eval_jaxpr/reshape | solution.py:79
  322.4 4.2 multiply_reduce_fusion.5
  327.3 28.1 %all-to-all-start.3 = ((f32[16,3,32]{2,1,0:T(4,128)}), f32[16,3,32]{2,1,0:T(4,128)S(1)}, u32[]{:S(2)}, u32[]{:S(2)}) async-start(f32[16,3,32]{2,1,0:T(4,128)} %all_to_all.24), calls=%async_computation.3 | async-start | bytes 65536 | tf_op jit(solution)/shard_map/all_to_all | solution.py:107
  355.5 6.5 %all-to-all-done.3 = f32[16,3,32]{2,1,0:T(4,128)S(1)} async-done(((f32[16,3,32]{2,1,0:T(4,128)}), f32[16,3,32]{2,1,0:T(4,128)S(1)}, u32[]{:S(2)}, u32[]{:S(2)}) %all-to-all-start.3) | async-done | bytes 6176 | tf_op jit(solution)/shard_map/all_to_all | solution.py:107
  362.6 5.2 %convolution_bitcast_fusion = f32[1024,1024]{0,1:T(8,128)} fusion(bf16[512,1024]{1,0:T(8,128)(2,1)} %bitcast.74, f32[512,1024]{1,0:T(8,128)} %get-tuple-element.101, f32[512]{0:T(512)S(1)} %bitcast_subtract_fusion, f32[1024]{0:T(1024)S(1)} %convert_element_type.71), kind=kOutput, calls=%fused_computation.32 | convolution fusion | flops 1075838976 | bytes 7346176 | tf_op jit(solution)/shard_map/dot_general | solution.py:126
  367.8 5.3 %copy.56 = f32[1024,1024]{1,0:T(8,128)} copy(f32[1024,1024]{0,1:T(8,128)} %convolution_bitcast_fusion) | data formatting | bytes 8388608
  373.2 70.1 %reduce-scatter.4.cloned.1.call-done = f32[64,1024]{1,0:T(8,128)} async-done(((f32[1024,1024]{1,0:T(8,128)}), f32[64,1024]{1,0:T(8,128)}) %reduce-scatter.4.cloned.1.call-update) | async-done | bytes 262160
  447.2 39.8 %psum.15 = f32[1024]{0:T(1024)} all-reduce(f32[1024]{0:T(1024)S(1)} %multiply_reduce_fusion.1), channel_id=1, replica_groups=mesh['group'=2,'shard'=16] {'group','shard'}, use_global_device_ids=true, to_apply=%region_15.16 | all-reduce | flops 1024 | bytes 8192 | tf_op jit(solution)/shard_map/psum | solution.py:134
  (111 shorter events, 65.6 us)
Async XLA Ops:
  7.2 98.1 %copy-start = (bf16[1024,1024]{1,0:T(8,128)(2,1)S(1)}, bf16[1024,1024]{1,0:T(8,128)(2,1)}, u32[]{:S(2)}) copy-start(bf16[1024,1024]{1,0:T(8,128)(2,1)} %param.18) | copy-start | bytes 6291460
  10.8 13.8 %all-to-all-start.1 = ((bf16[16,3,1]{1,2,0:T(2,128)(2,1)}), bf16[16,3,1]{1,2,0:T(2,128)(2,1)S(1)}, u32[]{:S(2)}, u32[]{:S(2)}) async-start(bf16[16,3,1]{1,2,0:T(2,128)(2,1)} %all_to_all.27), calls=%async_computation.1 | async-start | bytes 16384 | tf_op jit(solution)/shard_map/all_to_all | solution.py:59
  24.2 6.2 %copy-start.4 = (bf16[4,128,512]{2,1,0:T(8,128)(2,1)S(1)}, bf16[4,128,512]{2,1,0:T(8,128)(2,1)}, u32[]{:S(2)}) copy-start(bf16[4,128,512]{2,1,0:T(8,128)(2,1)} %param.17) | copy-start | bytes 1572868
  24.6 65.1 %all-to-all-start.2 = ((bf16[48,32,1024]{2,1,0:T(8,128)(2,1)}), bf16[48,32,1024]{2,1,0:T(8,128)(2,1)}, u32[]{:S(2)}, u32[]{:S(2)}) async-start(bf16[48,32,1024]{2,1,0:T(8,128)(2,1)} %copy.50), calls=%async_computation.2 | async-start | bytes 6291456 | tf_op jit(solution)/shard_map/all_to_all | solution.py:57
  38.6 66.6 %copy-start.7 = (bf16[1024]{0:T(1024)(128)(2,1)S(1)}, bf16[1024]{0:T(1024)(128)(2,1)}, u32[]{:S(2)}) copy-start(bf16[1024]{0:T(1024)(128)(2,1)} %param.19) | copy-start | bytes 6148
  38.6 66.7 %copy-start.3 = (bf16[4,128,1024]{2,1,0:T(8,128)(2,1)S(1)}, bf16[4,128,1024]{2,1,0:T(8,128)(2,1)}, u32[]{:S(2)}) copy-start(bf16[4,128,1024]{2,1,0:T(8,128)(2,1)} %param.13) | copy-start | bytes 3145732
  89.7 129.5 %all-to-all-start = ((bf16[48,128,512]{2,1,0:T(8,128)(2,1)}), bf16[48,128,512]{2,1,0:T(8,128)(2,1)}, u32[]{:S(2)}, u32[]{:S(2)}) async-start(bf16[48,128,512]{2,1,0:T(8,128)(2,1)} %copy.47), calls=%async_computation | async-start | bytes 12582912 | tf_op jit(solution)/shard_map/all_to_all | solution.py:58
  105.3 114.0 %copy-start.5 = (bf16[1,512]{1,0:T(2,128)(2,1)S(1)}, bf16[1,512]{1,0:T(2,128)(2,1)}, u32[]{:S(2)}) copy-start(bf16[1,512]{1,0:T(2,128)(2,1)} %param.23) | copy-start | bytes 3076
  219.3 143.1 %copy-start.6 = (s32[4,32]{1,0:T(4,128)S(1)}, s32[4,32]{1,0:T(4,128)}, u32[]{:S(2)}) copy-start(s32[4,32]{1,0:T(4,128)} %param.14) | copy-start | bytes 1540
  219.3 3.2 copy-start.10
  231.2 1.5 copy-start.8
  236.0 6.0 %copy-start.2 = (bf16[1,16,128,512]{3,2,1,0:T(8,128)(2,1)S(1)}, bf16[1,16,128,512]{3,2,1,0:T(8,128)(2,1)}, u32[]{:S(2)}) copy-start(bf16[1,16,128,512]{3,2,1,0:T(8,128)(2,1)} %copy-done.1) | copy-start | bytes 6291460 | tf_op jit(solution)/shard_map/while
  236.0 6.0 %copy-start.9 = (bf16[1,512,512]{2,1,0:T(8,128)(2,1)S(1)}, bf16[1,512,512]{2,1,0:T(8,128)(2,1)}, u32[]{:S(2)}) copy-start(bf16[1,512,512]{2,1,0:T(8,128)(2,1)} %get-tuple-element.184) | copy-start | bytes 1572868 | tf_op jit(solution)/shard_map/while
  255.1 3.2 copy-start.10
  267.0 1.5 copy-start.8
  271.8 6.0 %copy-start.2 = (bf16[1,16,128,512]{3,2,1,0:T(8,128)(2,1)S(1)}, bf16[1,16,128,512]{3,2,1,0:T(8,128)(2,1)}, u32[]{:S(2)}) copy-start(bf16[1,16,128,512]{3,2,1,0:T(8,128)(2,1)} %copy-done.1) | copy-start | bytes 6291460 | tf_op jit(solution)/shard_map/while
  271.8 6.0 %copy-start.9 = (bf16[1,512,512]{2,1,0:T(8,128)(2,1)S(1)}, bf16[1,512,512]{2,1,0:T(8,128)(2,1)}, u32[]{:S(2)}) copy-start(bf16[1,512,512]{2,1,0:T(8,128)(2,1)} %get-tuple-element.184) | copy-start | bytes 1572868 | tf_op jit(solution)/shard_map/while
  290.9 3.2 copy-start.10
  302.8 1.5 copy-start.8
  307.6 6.0 %copy-start.2 = (bf16[1,16,128,512]{3,2,1,0:T(8,128)(2,1)S(1)}, bf16[1,16,128,512]{3,2,1,0:T(8,128)(2,1)}, u32[]{:S(2)}) copy-start(bf16[1,16,128,512]{3,2,1,0:T(8,128)(2,1)} %copy-done.1) | copy-start | bytes 6291460 | tf_op jit(solution)/shard_map/while
  307.6 6.0 %copy-start.9 = (bf16[1,512,512]{2,1,0:T(8,128)(2,1)S(1)}, bf16[1,512,512]{2,1,0:T(8,128)(2,1)}, u32[]{:S(2)}) copy-start(bf16[1,512,512]{2,1,0:T(8,128)(2,1)} %get-tuple-element.184) | copy-start | bytes 1572868 | tf_op jit(solution)/shard_map/while
  327.3 34.7 %all-to-all-start.3 = ((f32[16,3,32]{2,1,0:T(4,128)}), f32[16,3,32]{2,1,0:T(4,128)S(1)}, u32[]{:S(2)}, u32[]{:S(2)}) async-start(f32[16,3,32]{2,1,0:T(4,128)} %all_to_all.24), calls=%async_computation.3 | async-start | bytes 65536 | tf_op jit(solution)/shard_map/all_to_all | solution.py:107
  355.4 88.0 %reduce-scatter.4.cloned.1.call-start = ((), (), s32[]{:S(2)}) async-start(), calls=%async_computation.6 | async-start | bytes 4456448
  373.1 113.8 %all-reduce.2.cloned.1.call-start = ((), (), s32[]{:S(2)}) async-start(), calls=%async_computation.5 | async-start | bytes 1048576 | tf_op jit(solution)/shard_map/psum | solution.py:133
  (3 other events, 3.9 us)
Sparse Core Ops, SparseCore 0:
  373.3 70.0 reduce-scatter.3
  445.6 28.0 all-reduce.1
where the time goes:
time: 497 us; the launch traced here: 496 us
  waiting for transfers between devices  239 us (48%)
  local copies, waits for them, and re-layouts  77.7 us (16%)
  matrix products  63.9 us (13%)
  starting transfers between devices  56.9 us (11%)
  blocking collectives  39.8 us (8%)
  between operations  14.2 us (3%)
    all_to_all x1, waiting for transfers between devices, body(): lax.all_to_all(send_hist, 'shard', split_axis=0, concat_axis=0, tiled=True)  111 us
    unnamed x3, waiting for transfers between devices  70.2 us
    all_to_all x1, waiting for transfers between devices, body(): lax.all_to_all(send_rows, 'shard', split_axis=0, concat_axis=0, tiled=True)  51.1 us
    psum x1, blocking collectives, body(): grad_score = lax.psum(local_score, ('group', 'shard'))  39.8 us
    all_to_all x1, starting transfers between devices, body(): lax.all_to_all(mentor_output, 'shard', split_axis=0, concat_axis=0, tiled...  28.1 us
    reshape x3, local copies, waits for them, and re-layouts, ranker_block(): key_rows.astype(jnp.bfloat16)  18.5 us
    reshape x3, local copies, waits for them, and re-layouts, ranker_block(): value_rows.astype(jnp.bfloat16)  18.5 us
    dot_general x3, matrix products, ranker_block(): jnp.einsum('skhd,sjhd->shkj', queries, key_rows, preferred_element_type=j...  17.9 us
  transfers between devices with their start and end apart: 6, of which 5 were waited for; matrix products, arithmetic and copies ran while one was open for 4% of the time, Pallas kernels for 0%

commit v1 on v0

v1 whole, which is shorter than its diff:
```python
import functools

import jax
import jax.numpy as jnp
from jax import lax
from jax.experimental import pallas as pl
from jax.experimental.pallas import tpu as pltpu
from jax.sharding import PartitionSpec as P

ATTENDER_GANGS = 8
META_ROWS = 16
VMEM = pltpu.VMEM
F32 = jnp.float32
BF16 = jnp.bfloat16


def full_vmem():
    return pl.BlockSpec(memory_space=pltpu.VMEM)


def rows_of(requests, hist_slots, kept, feature_span, focus_span):
    hist_rows = requests * hist_slots
    kept_rows = requests * kept
    pieces = feature_span // focus_span
    return hist_rows, kept_rows, pieces, hist_rows + kept_rows * pieces


def pack_kernel(x_ref, kept_ref, hist_ref, meta_ref, out_ref):
    requests, cand, _ = x_ref.shape
    kept = kept_ref.shape[1]
    focus = hist_ref.shape[1]
    hist_rows = hist_ref.shape[0]
    pieces = x_ref.shape[2] // focus
    out_ref[:hist_rows, :] = hist_ref[...]
    for r in range(requests):
        cand_of = lax.broadcasted_iota(jnp.int32, (cand, kept), 0)
        pick = (cand_of == kept_ref[r : r + 1, :]).astype(F32).astype(BF16)
        for p in range(pieces):
            rows = lax.dot_general(
                pick,
                x_ref[r, :, p * focus : (p + 1) * focus],
                (((0,), (0,)), ((), ())),
                preferred_element_type=F32,
            )
            at = hist_rows + p * requests * kept + r * kept
            out_ref[at : at + kept, :] = rows.astype(BF16)
    out_ref[hist_rows + pieces * requests * kept :, :] = meta_ref[...]


def pack(x, kept, hist, meta):
    requests, cand, feats = x.shape
    focus = hist.shape[2]
    flat_hist = hist.reshape(-1, focus)
    total = rows_of(requests, hist.shape[1], kept.shape[1], feats, focus)[3] + META_ROWS
    return pl.pallas_call(
        pack_kernel,
        out_shape=jax.ShapeDtypeStruct((total, focus), BF16),
        in_specs=[full_vmem()] * 4,
        out_specs=full_vmem(),
        cost_estimate=pl.CostEstimate(flops=10**8, bytes_accessed=3 * 10**6, transcendentals=0),
    )(x, kept, flat_hist, meta)


def student_kernel(requests, x_ref, w_ref, s_ref, grad_ref, gs_ref, part_ref):
    rows, feats = x_ref.shape
    units = w_ref.shape[1]
    cand = rows // requests
    score_vec = s_ref[...].astype(F32)

    def one(r, total):
        at = pl.ds(pl.multiple_of(r * cand, cand), cand)
        preact = jnp.dot(x_ref[at, :], w_ref[...], preferred_element_type=F32)
        hidden = jnp.maximum(preact, 0.0)
        exp_scores = jnp.exp(jnp.sum(hidden * score_vec, axis=-1, keepdims=True))
        student = exp_scores / jnp.sum(exp_scores, axis=0, keepdims=True)
        live = jnp.where(preact > 0, student * score_vec, 0.0)
        part_ref[at, :] = live.astype(BF16)
        return total + jnp.sum(student * hidden, axis=0, keepdims=True)

    gs_ref[...] = lax.fori_loop(0, requests, one, jnp.zeros((1, units), F32))
    step = min(256, feats)

    def block(i, carry):
        at = pl.ds(pl.multiple_of(i * step, step), step)
        grad_ref[at, :] = lax.dot_general(
            x_ref[:, at], part_ref[...], (((0,), (0,)), ((), ())), preferred_element_type=F32
        )
        return carry

    lax.fori_loop(0, feats // step, block, 0)


def student_part(x, w, s):
    requests, cand, feats = x.shape
    units = w.shape[1]
    return pl.pallas_call(
        functools.partial(student_kernel, requests),
        out_shape=(
            jax.ShapeDtypeStruct((feats, units), F32),
            jax.ShapeDtypeStruct((1, units), F32),
        ),
        in_specs=[full_vmem()] * 3,
        out_specs=(full_vmem(), full_vmem()),
        scratch_shapes=[VMEM((requests * cand, units), BF16)],
        cost_estimate=pl.CostEstimate(
            flops=4 * requests * cand * feats * units, bytes_accessed=8 * 10**6, transcendentals=0
        ),
    )(x.reshape(requests * cand, feats), w, s.reshape(1, units))


def rank_block(dims, me, payload, ask, look, rate, w, sel_rows):
    requests, hist_slots, kept, tops, gangs = dims
    focus = look.shape[0]
    span = look.shape[1] // gangs
    hist_rows, kept_rows, pieces, meta_at = rows_of(
        requests, hist_slots, kept, ask.shape[0], focus
    )
    hist = payload[:hist_rows, :]
    keys = jnp.dot(hist, look[...], preferred_element_type=F32).astype(BF16)
    values = jnp.dot(hist, rate[...], preferred_element_type=F32)
    queries = jnp.zeros((kept_rows, look.shape[1]), F32)
    preact = jnp.zeros((kept_rows, w.shape[1]), F32)
    own = jnp.zeros((sel_rows, kept_rows), F32)
    for p in range(pieces):
        rows = payload[hist_rows + p * kept_rows : hist_rows + (p + 1) * kept_rows, :]
        at = slice(p * focus, (p + 1) * focus)
        queries += jnp.dot(rows, ask[at, :], preferred_element_type=F32)
        preact += jnp.dot(rows, w[at, :], preferred_element_type=F32)
        feature = lax.broadcasted_iota(jnp.int32, (sel_rows, focus), 1) + p * focus
        wanted = lax.broadcasted_iota(jnp.int32, (sel_rows, focus), 0) + me * sel_rows
        pick = (feature == wanted).astype(F32).astype(BF16)
        own += lax.dot_general(pick, rows, (((1,), (1,)), ((), ())), preferred_element_type=F32)
    queries = (queries * span**-0.5).astype(BF16)
    hidden = jnp.maximum(preact, 0.0).astype(BF16)
    wide = gangs * kept
    head_row = lax.broadcasted_iota(jnp.int32, (wide, look.shape[1]), 0) // kept
    head_col = lax.broadcasted_iota(jnp.int32, (wide, look.shape[1]), 1) // span
    same_head = head_row == head_col
    slot = lax.broadcasted_iota(jnp.int32, (hist_slots, wide), 0).astype(F32)
    meta = payload[meta_at : meta_at + META_ROWS, :].astype(F32)
    meta_lane = lax.broadcasted_iota(jnp.int32, meta.shape, 1)
    hit = jnp.where((meta_lane < tops) & (meta == me.astype(F32)), 1.0, 0.0)
    routed = jnp.max(hit, axis=-1, keepdims=True)
    lengths = jnp.sum(jnp.where(meta_lane == tops, meta, 0.0), axis=-1, keepdims=True)
    lane = lax.broadcasted_iota(jnp.int32, (1, kept_rows), 1) // kept
    scores = jnp.zeros((1, kept_rows), F32)
    for r in range(requests):
        q = queries[r * kept : (r + 1) * kept, :]
        q_wide = jnp.where(same_head, jnp.concatenate([q] * gangs, axis=0), jnp.zeros((), BF16))
        logits = lax.dot_general(
            keys[r * hist_slots : (r + 1) * hist_slots, :],
            q_wide,
            (((1,), (1,)), ((), ())),
            preferred_element_type=F32,
        )
        weights = jnp.where(slot < lengths[r : r + 1, :], jnp.exp(logits), 0.0)
        mixed = weights * values[r * hist_slots : (r + 1) * hist_slots, :]
        per_head = jnp.sum(mixed, axis=0, keepdims=True) / jnp.sum(weights, axis=0, keepdims=True)
        folded = per_head[:, :kept_rows]
        for b in range(1, wide // kept_rows):
            folded = folded + per_head[:, b * kept_rows : (b + 1) * kept_rows]
        shift = kept
        while shift < kept_rows:
            folded = folded + pltpu.roll(folded, shift, 1)
            shift *= 2
        scores = jnp.where(lane == r, folded * routed[r : r + 1, :], scores)
    return scores, hidden, own.astype(BF16)


def rank_kernel(dims, sel_rows, me_ref, p_ref, a_ref, l_ref, r_ref, w_ref, o_ref, h_ref, s_ref):
    scores, hidden, own = rank_block(
        dims, me_ref[0], p_ref.at[0], a_ref, l_ref, r_ref, w_ref, sel_rows
    )
    o_ref[0] = scores
    h_ref[...] = hidden
    s_ref[...] = own


def rank(dims, me, payloads, ask, look, rate, w, sel_rows):
    blocks, rows, focus = payloads.shape
    requests, hist_slots, kept, _, _ = dims
    kept_rows = requests * kept
    units = w.shape[1]
    hold = dict(pipeline_mode=pl.Buffered(1))
    return pl.pallas_call(
        functools.partial(rank_kernel, dims, sel_rows),
        out_shape=(
            jax.ShapeDtypeStruct((blocks, 1, kept_rows), F32),
            jax.ShapeDtypeStruct((blocks * kept_rows, units), BF16),
            jax.ShapeDtypeStruct((sel_rows, blocks * kept_rows), BF16),
        ),
        grid=(blocks,),
        in_specs=[
            pl.BlockSpec(memory_space=pltpu.SMEM),
            pl.BlockSpec((1, rows, focus), lambda b: (b, 0, 0)),
            pl.BlockSpec(ask.shape, lambda b: (0, 0), **hold),
            pl.BlockSpec(look.shape, lambda b: (0, 0), **hold),
            pl.BlockSpec(rate.shape, lambda b: (0, 0), **hold),
            pl.BlockSpec(w.shape, lambda b: (0, 0), **hold),
        ],
        out_specs=(
            pl.BlockSpec((1, 1, kept_rows), lambda b: (b, 0, 0)),
            pl.BlockSpec((kept_rows, units), lambda b: (b, 0)),
            pl.BlockSpec((sel_rows, kept_rows), lambda b: (0, b)),
        ),
        cost_estimate=pl.CostEstimate(
            flops=blocks * 10**9, bytes_accessed=blocks * 10**6, transcendentals=0
        ),
    )(me, payloads, ask, look, rate, w)


def target_kernel(kept, tops, got_ref, hid_ref, sel_ref, s_ref, base_ref, out_ref):
    blocks, kept_rows = got_ref.shape[1] - s_ref.shape[1] // got_ref.shape[2], got_ref.shape[2]
    sel_rows = sel_ref.shape[0]
    units = s_ref.shape[1]
    total = jnp.sum(got_ref[...], axis=0)
    exp_teacher = jnp.exp(total[:blocks, :] / tops)
    near = lax.broadcasted_iota(jnp.int32, (kept_rows, kept_rows), 0) // kept
    far = lax.broadcasted_iota(jnp.int32, (kept_rows, kept_rows), 1) // kept
    group = (near == far).astype(F32)
    sums = jnp.dot(
        exp_teacher, group, preferred_element_type=F32, precision=lax.Precision.HIGHEST
    )
    target = exp_teacher / sums
    high = target.astype(BF16)
    low = (target - high.astype(F32)).astype(BF16)
    grad = jnp.zeros((sel_rows, units), F32)
    lift = jnp.zeros((1, units), F32)
    for b in range(blocks):
        at = slice(b * kept_rows, (b + 1) * kept_rows)
        hidden = hid_ref[at, :]
        live = jnp.where(hidden > 0, jnp.ones((), BF16), jnp.zeros((), BF16))
        scaled = (sel_ref[:, at].astype(F32) * target[b : b + 1, :]).astype(BF16)
        grad += jnp.dot(scaled, live, preferred_element_type=F32)
        both = jnp.concatenate([high[b : b + 1, :], low[b : b + 1, :]], axis=0)
        pair = jnp.dot(both, hidden, preferred_element_type=F32)
        lift += pair[0:1, :] + pair[1:2, :]
    out_ref[:sel_rows, :] = base_ref[...] - grad * s_ref[...].astype(F32)
    lanes = got_ref.shape[2]
    for i in range(units // lanes):
        at = slice(i * lanes, (i + 1) * lanes)
        out_ref[sel_rows : sel_rows + 1, at] = total[blocks + i : blocks + i + 1, :] - lift[:, at]
    out_ref[sel_rows + 1 :, :] = jnp.zeros((out_ref.shape[0] - sel_rows - 1, units), F32)


def target_part(kept, tops, got, hidden, own, s, base):
    sel_rows = own.shape[0]
    units = hidden.shape[1]
    return pl.pallas_call(
        functools.partial(target_kernel, kept, tops),
        out_shape=jax.ShapeDtypeStruct((sel_rows + 8, units), F32),
        in_specs=[full_vmem()] * 5,
        out_specs=full_vmem(),
        cost_estimate=pl.CostEstimate(flops=10**9, bytes_accessed=6 * 10**6, transcendentals=0),
    )(got, hidden, own, s.reshape(1, units), base)


def body(
    offer_attribute_matrix,
    kept_offers,
    expert_target,
    sequence_extent,
    behaviour_sequence,
    inner_projection_matrix,
    student_rating_vector,
    asking_matrix,
    lookup_matrix,
    content_matrix,
    expert_rating_vector,
):
    requests, _, feats = offer_attribute_matrix.shape
    kept = kept_offers.shape[1]
    hist_slots, focus = behaviour_sequence.shape[1:]
    tops = expert_target.shape[1]
    units = inner_projection_matrix.shape[1]
    n_shard = lax.axis_size("shard")
    sel_rows = feats // n_shard
    kept_rows = requests * kept
    me = lax.axis_index("shard")

    meta = jnp.concatenate([expert_target, sequence_extent[:, None]], axis=1).astype(BF16)
    meta = jnp.pad(meta, ((0, META_ROWS - requests), (0, focus - tops - 1)))
    payload = pack(offer_attribute_matrix, kept_offers, behaviour_sequence, meta)
    payloads = lax.all_gather(payload, "shard", axis=0, tiled=False)

    grad_student, gs_student = student_part(
        offer_attribute_matrix, inner_projection_matrix, student_rating_vector
    )
    base = lax.psum_scatter(grad_student, "shard", scatter_dimension=0, tiled=True)

    head_of = jnp.arange(focus, dtype=jnp.int32)[:, None] // (focus // ATTENDER_GANGS)
    lane_head = jnp.arange(ATTENDER_GANGS * kept, dtype=jnp.int32)[None, :] // kept
    rated = content_matrix[0].astype(F32) * expert_rating_vector[0].astype(F32)
    rate = jnp.dot(
        rated, (head_of == lane_head).astype(F32), precision=lax.Precision.HIGHEST
    ).astype(BF16)

    dims = (requests, hist_slots, kept, tops, ATTENDER_GANGS)
    scores, hidden, own = rank(
        dims,
        me.reshape(1).astype(jnp.int32),
        payloads,
        asking_matrix[0],
        lookup_matrix[0],
        rate,
        inner_projection_matrix,
        sel_rows,
    )
    lanes = kept_rows
    send = jnp.concatenate([scores.reshape(-1, lanes), gs_student.reshape(-1, lanes)], axis=0)
    send = jnp.broadcast_to(send[None], (n_shard,) + send.shape)
    got = lax.all_to_all(send, "shard", split_axis=0, concat_axis=0, tiled=True)
    mine = target_part(kept, tops, got, hidden, own, student_rating_vector, base)
    whole = lax.psum(mine, "group")
    return whole[:sel_rows], whole[sel_rows]


def solution(mesh):
    placed = (
        P(("group", "shard"), None, None),
        P(("group", "shard"), None),
        P(("group", "shard"), None),
        P(("group", "shard")),
        P(("group", "shard"), None, None),
        P(),
        P(),
        P("shard", None, None),
        P("shard", None, None),
        P("shard", None, None),
        P("shard", None),
    )
    return jax.shard_map(
        body, mesh=mesh, in_specs=placed, out_specs=(P("shard", None), P()), check_vma=False
    )
```

time: 497 us -> 232 us (0.47)
  waiting for transfers between devices: 239 us -> 160 us
  local copies, waits for them, and re-layouts: 77.7 us -> 5.79 us
  matrix products: 63.9 us -> 1.49 us
  starting transfers between devices: 56.9 us -> 3.64 us
  Pallas kernels: 0 us -> 44.7 us
  blocking collectives: 39.8 us -> 0 us
    all_to_all x4 -> x1, waiting for transfers between devices: 169 us -> 0.01 us  [body(): got = lax.all_to_all(send, 'shard', split_axis=0, concat_axis=0, tiled=True)]
    all_gather x0 -> x1, waiting for transfers between devices: none -> 93.3 us  [body(): payloads = lax.all_gather(payload, 'shard', axis=0, tiled=False)]
    unnamed x3, waiting for transfers between devices: 70.2 us -> 0.05 us
    dot_general x22 -> x1, matrix products: 63.9 us -> 1.49 us  [body(): jnp.dot(rated, (head_of == lane_head).astype(F32), precision=lax.Precisio...]
    all_to_all x4 -> x1, starting transfers between devices: 56.8 us -> 3.52 us  [body(): got = lax.all_to_all(send, 'shard', split_axis=0, concat_axis=0, tiled=True)]
    pallas_call x0 -> x4, Pallas kernels: none -> 44.7 us  [the longest x1 28.7 us: rank(): pl.pallas_call(functools.partial(rank_kernel, dims, sel_rows), out_shape=...]
    reduce_scatter x0 -> x1, waiting for transfers between devices: none -> 43.4 us  [body(): lax.psum_scatter(grad_student, 'shard', scatter_dimension=0, tiled=True)]
    reshape x10 -> x1, local copies, waits for them, and re-layouts: 42 us -> 1.28 us  [student_part(): s.reshape(1, units)]
  transfers between devices with their start and end apart: 6 -> 4, of which waited for: 5 -> 3; matrix products, arithmetic and copies ran while one was open for 4% -> 2% of each run, Pallas kernels for 0% -> 16%
where the time goes in v1:
time: 232 us
  waiting for transfers between devices  160 us (69%)
  Pallas kernels  44.7 us (19%)
  between operations  13.8 us (6%)
  local copies, waits for them, and re-layouts  5.79 us (2%)
  starting transfers between devices  3.64 us (2%)
  other arithmetic  2.74 us (1%)
    all_gather x1, waiting for transfers between devices, body(): payloads = lax.all_gather(payload, 'shard', axis=0, tiled=False)  93.3 us
    reduce_scatter x1, waiting for transfers between devices, body(): lax.psum_scatter(grad_student, 'shard', scatter_dimension=0, tiled=True)  43.4 us
    pallas_call x1, Pallas kernels, rank(): pl.pallas_call(functools.partial(rank_kernel, dims, sel_rows), out_shape=...  28.7 us
    psum x1, waiting for transfers between devices, body(): whole = lax.psum(mine, 'group')  22.9 us
    pallas_call x1, Pallas kernels, student_part(): pl.pallas_call(functools.partial(student_kernel, requests), out_shape=(ja...  8.69 us
    pallas_call x1, Pallas kernels, target_part(): pl.pallas_call(functools.partial(target_kernel, kept, tops), out_shape=ja...  4.67 us
  transfers between devices with their start and end apart: 4, of which 3 were waited for; matrix products, arithmetic and copies ran while one was open for 2% of the time, Pallas kernels for 16%

profile of v1, /device:TPU:0, one launch (start us, length us, event | category | flops | bytes accessed | tf_op | source)
XLA Modules:
  0.0 231.8 jit_solution(7940572834189892456)
XLA Ops:
  7.2 0.0 all-gather.3.cloned.1.call-start
  7.2 0.7 convert_bitcast_fusion
  7.9 0.1 copy.13
  8.0 0.7 convert.9
  8.7 0.7 fusion.10.meta_ref
  9.3 2.6 %shard_map.122 = bf16[784,512]{1,0:T(8,128)(2,1)} custom-call(bf16[4,128,1024]{2,1,0:T(8,128)(2,1)} %x_ref.1, s32[4,32]{1,0:T(4,128)} %kept_ref.1, bf16[512,512]{1,0:T(8,128)(2,1)} %bitcast.19, bf16[16,512]{1,0:T(8,128)(2,1)} %fusion.10.meta_ref), custom_call_target="tpu_custom_call" | custom-call | flops 100000000 | bytes 3000000 | tf_op jit(solution)/shard_map/pallas_call | solution.py:55
  11.9 0.0 all-gather.3.cloned.1.call-update
  12.0 0.0 reduce-scatter.2.cloned.1.call-start
  12.0 1.3 reshape.104.s_ref
  13.3 8.7 %shard_map.124 = (f32[1024,1024]{1,0:T(8,128)}, f32[1,1024]{1,0:T(1,128)}) custom-call(bf16[512,1024]{1,0:T(8,128)(2,1)} %bitcast.18, bf16[1024,1024]{1,0:T(8,128)(2,1)} %w_ref.3, bf16[1,1024]{1,0:T(2,128)(2,1)} %reshape.104.s_ref), custom_call_target="tpu_custom_call" | custom-call | flops 2147483648 | bytes 8000000 | tf_op jit(solution)/shard_map/pallas_call | solution.py:96
  22.0 0.0 reduce-scatter.2.cloned.1.call-update
  22.1 1.5 convolution_convert_fusion.r_ref
  23.6 93.3 %all-gather.3.cloned.1.call-done = bf16[12544,512]{1,0:T(8,128)(2,1)} async-done(((bf16[784,512]{1,0:T(8,128)(2,1)}), bf16[12544,512]{1,0:T(8,128)(2,1)}) %all-gather.3.cloned.1.call-update) | async-done | bytes 12845072 | tf_op jit(solution)/shard_map/all_gather | solution.py:284
  116.9 28.7 %shard_map.123 = (f32[16,1,128]{2,1,0:T(1,128)}, bf16[2048,1024]{1,0:T(8,128)(2,1)}, bf16[64,2048]{1,0:T(8,128)(2,1)}) custom-call(s32[1]{0:T(128)} %bitcast.me_ref, bf16[16,784,512]{2,1,0:T(8,128)(2,1)} %bitcast.24, bf16[1024,512]{1,0:T(8,128)(2,1)} %bitcast.25, bf16[512,512]{1,0:T(8,128)(2,1)} %bitcast.26, bf16[512,256]{1,0:T(8,128)(2,1)} %convolution_convert_fusion.r_ref, ...), custom_call_target="tpu_custom_call" | custom-call | flops 16000000000 | bytes 16000000 | tf_op jit(solution)/shard_map/pallas_call | solution.py:185
  145.6 0.7 pad_maximum_fusion
  146.3 0.7 broadcast_in_dim.6
  147.0 3.5 %all-to-all-start = ((f32[16,24,128]{2,1,0:T(8,128)}), f32[16,24,128]{2,1,0:T(8,128)S(1)}, u32[]{:S(2)}, u32[]{:S(2)}) async-start(f32[16,24,128]{2,1,0:T(8,128)} %broadcast_in_dim.6), calls=%async_computation | async-start | bytes 393216 | tf_op jit(solution)/shard_map/all_to_all | solution.py:312
  150.5 0.0 all-reduce.3.cloned.1.call-start
  150.6 43.4 %reduce-scatter.2.cloned.1.call-done.base_ref = f32[64,1024]{1,0:T(8,128)} async-done(((f32[1024,1024]{1,0:T(8,128)}), f32[64,1024]{1,0:T(8,128)}) %reduce-scatter.2.cloned.1.call-update) | async-done | bytes 262160 | tf_op jit(solution)/shard_map/reduce_scatter | solution.py:289
  193.9 0.7 copy-done
  194.6 4.7 %shard_map.125 = f32[72,1024]{1,0:T(8,128)} custom-call(f32[16,24,128]{2,1,0:T(8,128)} %copy-done, bf16[2048,1024]{1,0:T(8,128)(2,1)} %get-tuple-element.9.hid_ref, bf16[64,2048]{1,0:T(8,128)(2,1)} %get-tuple-element.10.sel_ref, bf16[1,1024]{1,0:T(2,128)(2,1)} %reshape.104.s_ref, f32[64,1024]{1,0:T(8,128)} %reduce-scatter.2.cloned.1.call-done.base_ref), custom_call_target="tpu_custom_call" | custom-call | flops 1000000000 | bytes 6000000 | tf_op jit(solution)/shard_map/pallas_call | solution.py:249
  199.3 22.9 %all-reduce.3.cloned.1.call-done = f32[72,1024]{1,0:T(8,128)} async-done(((f32[72,1024]{1,0:T(8,128)}), f32[72,1024]{1,0:T(8,128)}) %all-reduce.3.cloned.1.call-update) | async-done | bytes 294928 | tf_op jit(solution)/shard_map/psum | solution.py:314
  222.2 1.7 slice.8
  223.9 1.4 slice.9
  (12 shorter events, 0.0 us)
Async XLA Ops:
  7.2 109.7 %all-gather.3.cloned.1.call-start = ((), (), s32[]{:S(2)}) async-start(), calls=%async_computation.4 | async-start | bytes 13647872 | tf_op jit(solution)/shard_map/all_gather | solution.py:284
  12.0 182.0 %reduce-scatter.2.cloned.1.call-start = ((), (), s32[]{:S(2)}) async-start(), calls=%async_computation.2 | async-start | bytes 4456448 | tf_op jit(solution)/shard_map/reduce_scatter | solution.py:289
  13.3 8.7 %copy-start.2 = (bf16[1,512]{1,0:T(2,128)(2,1)S(1)}, bf16[1,512]{1,0:T(2,128)(2,1)}, u32[]{:S(2)}) copy-start(bf16[1,512]{1,0:T(2,128)(2,1)} %param.21) | copy-start | bytes 3076
  13.3 8.8 %copy-start.3 = (bf16[1,512,512]{2,1,0:T(8,128)(2,1)S(1)}, bf16[1,512,512]{2,1,0:T(8,128)(2,1)}, u32[]{:S(2)}) copy-start(bf16[1,512,512]{2,1,0:T(8,128)(2,1)} %param.20) | copy-start | bytes 1572868
  116.9 28.7 %copy-start.1 = (f32[1,1024]{1,0:T(1,128)S(1)}, f32[1,1024]{1,0:T(1,128)}, u32[]{:S(2)}) copy-start(f32[1,1024]{1,0:T(1,128)} %get-tuple-element.8) | copy-start | bytes 12292
  147.0 47.0 %all-to-all-start = ((f32[16,24,128]{2,1,0:T(8,128)}), f32[16,24,128]{2,1,0:T(8,128)S(1)}, u32[]{:S(2)}, u32[]{:S(2)}) async-start(f32[16,24,128]{2,1,0:T(8,128)} %broadcast_in_dim.6), calls=%async_computation | async-start | bytes 393216 | tf_op jit(solution)/shard_map/all_to_all | solution.py:312
  150.5 71.7 %all-reduce.3.cloned.1.call-start = ((), (), s32[]{:S(2)}) async-start(), calls=%async_computation.3 | async-start | bytes 589824 | tf_op jit(solution)/shard_map/psum | solution.py:314
  193.9 0.7 copy-start
Sparse Core Ops, SparseCore 0:
  12.1 104.7 all-gather.2
  120.7 73.1 reduce-scatter.1
  199.4 22.7 all-reduce.2
